TPU v7x, 512 devices: a whole 4x4x16 slice. The times are simulated.
512 devices in a mesh: guide: 2 (over x_lo), seq: 32 (over x_hi, z), blk: 8 (over y, core).
Axes of the slice: x: 4 (x_hi: 2, x_lo: 2; x = x_hi * 2 + x_lo), y: 4, z: 16, core: 2. Of those that a mesh axis runs over, the one named last changes fastest.
Arguments:
- img_hidden: bfloat16 [2, 2, 2048, 3072], P('guide', None, 'seq', 'blk'), may hold values from -6 to 6
- img_query: bfloat16 [2, 2, 2048, 3072], P('guide', None, 'seq', 'blk')
- img_key: bfloat16 [2, 2, 2048, 3072], P('guide', None, 'seq', 'blk')
- img_value: bfloat16 [2, 2, 2048, 3072], P('guide', None, 'seq', 'blk'), may hold values from -6 to 6
- txt_key: bfloat16 [2, 2, 512, 3072], P('guide', None, 'seq', 'blk'), may hold values from -6 to 6
- txt_value: bfloat16 [2, 2, 512, 3072], P('guide', None, 'seq', 'blk'), may hold values from -6 to 6
- query_gain: float32 [128], replicated
- key_gain: float32 [2, 128], replicated
- gate: float32 [2, 2, 3072], P('guide', None, 'blk'), may hold values from -4 to 4
- proj_weight: bfloat16 [3072, 3072], P('blk'), may hold values from -0.15625 to 0.15625
- proj_bias: float32 [3072], P('blk'), may hold values from -3 to 3
- guidance: float32 [2], replicated, may hold values from 1.5 to 5
- text_len: int32 [2], replicated, may hold values from 1 to 512, as said below
- step_index: int32 [1], replicated, may hold values from 0 to 7
- latent: bfloat16 [2, 2048, 3072], P('guide', 'seq', 'blk'), may hold values from -6 to 6
Outputs:
- guided: bfloat16 [2, 2048, 3072], P('guide', 'seq', 'blk')
- next_state: bfloat16 [2, 2048, 3072], P('guide', 'seq', 'blk')
Inputs may be any that keep to these rules, and one draw needn't show every extreme that they name: `text_len`: some prompt has all 512 text slots live.
All inputs are finite; a program needn't handle non-finite values.
Results may differ from a plain program's by a relative error of at most 0.0095.
Values may be sent and summed in bfloat16 or wider, within the bound.
No kernel may reach another device: no remote copies, remote signals or barrier semaphores. Data moves between devices by JAX's collectives and lax.ppermute only.
A program may use at most 64 MiB of HBM per device.

v0:
```python
import jax
import jax.numpy as jnp
from jax import lax
from jax.sharding import PartitionSpec as P

HD = 128
GRID = 64
STEPS = 8


def rope_angles(positions):
    first = HD // 8
    second = (HD - first) // 2
    freqs = 10000.0 ** (-jnp.arange(0, second, 2).astype(jnp.float32) / second)
    rows = (positions // GRID).astype(jnp.float32)
    cols = (positions % GRID).astype(jnp.float32)
    zeros = jnp.zeros((positions.shape[0], first // 2), jnp.float32)
    return jnp.concatenate([zeros, rows[:, None] * freqs, cols[:, None] * freqs], -1)


def rotate(values, angles):
    pairs = values.reshape(values.shape[:-1] + (HD // 2, 2))
    cosine = jnp.cos(angles)[None, :, None, :]
    sine = jnp.sin(angles)[None, :, None, :]
    first = pairs[..., 0] * cosine - pairs[..., 1] * sine
    second = pairs[..., 0] * sine + pairs[..., 1] * cosine
    return jnp.stack([first, second], -1).reshape(values.shape)


def normed(values, gain_row):
    heads = values.astype(jnp.float32).reshape(
        values.shape[0], values.shape[1], values.shape[2] // HD, HD
    )
    return heads / jnp.sqrt(jnp.mean(heads * heads, -1, keepdims=True) + 1e-06) * gain_row


def shards(
    img_hidden,
    img_query,
    img_key,
    img_value,
    txt_key,
    txt_value,
    query_gain,
    key_gain,
    gate,
    proj_weight,
    proj_bias,
    guidance,
    text_len,
    step_index,
    latent,
):
    prompts = img_query.shape[1]
    img_here = img_query.shape[2]
    txt_here = txt_key.shape[2]
    width_here = img_query.shape[3]
    heads_here = width_here // HD
    slot_here = img_here + txt_here
    positions = lax.axis_index("seq") * img_here + jnp.arange(img_here)
    angles = rope_angles(positions)
    queries = rotate(normed(img_query[0], query_gain), angles).astype(jnp.bfloat16)
    keys_img = rotate(normed(img_key[0], key_gain[0]), angles).astype(jnp.bfloat16)
    keys_txt = normed(txt_key[0], key_gain[1]).astype(jnp.bfloat16)
    keys_local = jnp.concatenate([keys_txt, keys_img], 1).reshape(prompts, slot_here, width_here)
    values_local = jnp.concatenate([txt_value[0], img_value[0]], 1)
    running = jnp.full((prompts, img_here, heads_here), -1e30, jnp.float32)
    key_piece = lax.all_gather(keys_local, "seq", axis=1, tiled=True)
    value_piece = lax.all_gather(values_local, "seq", axis=1, tiled=True)
    count = key_piece.shape[1]
    index = jnp.arange(count)
    device = index // slot_here
    within = index % slot_here
    text_pos = device * txt_here + within
    live = (within >= txt_here)[None, :] | (text_pos[None, :] < text_len[:, None])
    key_heads = key_piece.reshape(prompts, count, heads_here, HD)
    value_heads = value_piece.reshape(prompts, count, heads_here, HD)
    scores = jnp.einsum(
        "pqhd,pkhd->pqhk", queries, key_heads, preferred_element_type=jnp.float32
    ) * HD ** (-0.5)
    mask = live[:, None, None, :]
    scores = jnp.where(mask, scores, -1e30)
    newest = jnp.maximum(running, jnp.max(scores, -1))
    expo = jnp.where(mask, jnp.exp(scores - newest[..., None]), 0.0)
    total = jnp.sum(expo, -1)
    accum = jnp.einsum(
        "pqhk,pkhd->pqhd",
        expo.astype(jnp.bfloat16),
        value_heads,
        preferred_element_type=jnp.float32,
    )
    running, total, accum = (newest, total, accum)
    attn = (accum / total[..., None]).astype(jnp.bfloat16).reshape(prompts * img_here, width_here)
    partial_value = jnp.dot(attn, proj_weight, preferred_element_type=jnp.float32)
    proj = lax.psum_scatter(
        partial_value.astype(jnp.bfloat16), "blk", scatter_dimension=1, tiled=True
    ).astype(jnp.float32)
    proj = (proj + proj_bias).reshape(prompts, img_here, width_here)
    layer_out = (img_hidden[0].astype(jnp.float32) + gate[0][:, None, :] * proj).astype(
        jnp.bfloat16
    )
    both_halves = lax.all_to_all(layer_out[None], "guide", split_axis=1, concat_axis=0, tiled=True)
    cond = both_halves[0].astype(jnp.float32)
    uncond = both_halves[1].astype(jnp.float32)
    own_prompts = cond.shape[0]
    scale_here = lax.dynamic_slice_in_dim(
        guidance, lax.axis_index("guide") * own_prompts, own_prompts, 0
    )
    guided_f = uncond + scale_here[:, None, None] * (cond - uncond)
    index = step_index[0]
    u_now = 1.0 - index.astype(jnp.float32) / STEPS
    u_next = 1.0 - (index + 1).astype(jnp.float32) / STEPS
    step_size = 3.0 * u_next / (1.0 + 2.0 * u_next) - 3.0 * u_now / (1.0 + 2.0 * u_now)
    next_state = (latent.astype(jnp.float32) + step_size * guided_f).astype(jnp.bfloat16)
    return (guided_f.astype(jnp.bfloat16), next_state)


def solution(mesh):
    return jax.shard_map(
        shards,
        mesh=mesh,
        in_specs=(
            P("guide", None, "seq", "blk"),
            P("guide", None, "seq", "blk"),
            P("guide", None, "seq", "blk"),
            P("guide", None, "seq", "blk"),
            P("guide", None, "seq", "blk"),
            P("guide", None, "seq", "blk"),
            P(),
            P(),
            P("guide", None, "blk"),
            P("blk", None),
            P("blk"),
            P(),
            P(),
            P(),
            P("guide", "seq", "blk"),
        ),
        out_specs=(P("guide", "seq", "blk"), P("guide", "seq", "blk")),
        check_vma=False,
    )
```

profile of v0, /device:TPU:4, one launch (start us, length us, event | category | flops | bytes accessed | tf_op | source)
XLA Modules:
  0.0 420.7 jit_solution(10959240967538015908)
XLA Ops:
  7.2 0.0 copy-start
  7.2 0.0 copy-start.4
  7.2 0.0 all-gather.5.cloned.1.call-start
  7.2 0.6 multiply_power_fusion
  7.8 1.6 convert_multiply_fusion.1
  9.5 1.0 copy.58
  10.5 1.6 convert_multiply_fusion.2
  12.1 1.0 copy.52
  13.1 0.6 fusion.35
  13.7 0.8 slice_bitcast_fusion.2
  14.5 0.1 mul.268
  14.6 1.0 mul.267
  15.6 0.2 reduce_sum.37
  15.9 0.7 copy.54
  16.6 1.0 mul.285
  17.6 0.2 reduce_sum.38
  17.8 0.0 copy-start.2
  17.8 0.7 copy.60
  18.5 0.8 mul.286
  19.3 0.7 convert_multiply_fusion
  20.1 0.1 reduce_sum.36
  20.2 0.1 div.91
  20.3 0.0 copy-done.4
  20.4 0.2 copy.55
  20.6 0.8 broadcast_multiply_fusion.1
  21.3 0.2 fusion.26
  21.5 1.1 divide_multiply_fusion
  22.7 1.0 subtract_convert_fusion
  23.7 0.5 pad_maximum_fusion
  24.2 0.1 pad_maximum_fusion.1
  24.4 0.8 copy.56
  25.2 0.0 all-gather.5.cloned.1.call-update
  25.2 0.0 all-gather.3.cloned.1.call-start
  25.2 0.1 copy.82
  25.4 0.8 copy.83
  26.1 0.8 pad_maximum_fusion.3
  26.9 0.0 all-gather.3.cloned.1.call-update
  27.0 0.0 reduce-scatter.4.cloned.1.call-start
  27.0 0.5 pad_maximum_fusion.2
  27.6 0.7 compare_or_fusion
  28.3 161.3 %all-gather.5.cloned.1.call-done = bf16[2,2560,384]{2,0,1:T(2,128)(2,1)} async-done(((bf16[2,80,384]{2,0,1:T(2,128)(2,1)}), bf16[2,2560,384]{2,0,1:T(2,128)(2,1)}) %all-gather.5.cloned.1.call-update) | async-done | bytes 3932176 | tf_op jit(solution)/shard_map/all_gather | solution.py:68
  189.6 10.5 %copy.57 = bf16[2,2560,384]{1,2,0:T(8,128)(2,1)} copy(bf16[2,2560,384]{2,0,1:T(2,128)(2,1)} %all-gather.5.cloned.1.call-done) | data formatting | bytes 7864320 | tf_op jit(solution)/shard_map/all_gather | solution.py:68
  200.1 3.2 fusion.38
  203.4 1.9 copy-done.1
  205.2 0.9 fusion.2
  206.1 143.7 %all-gather.3.cloned.1.call-done = bf16[2,2560,384]{2,0,1:T(2,128)(2,1)} async-done(((bf16[2,80,384]{2,0,1:T(2,128)(2,1)}), bf16[2,2560,384]{2,0,1:T(2,128)(2,1)}) %all-gather.3.cloned.1.call-update) | async-done | bytes 3932176 | tf_op jit(solution)/shard_map/all_gather | solution.py:69
  349.8 10.5 %copy.51 = bf16[2,2560,384]{1,2,0:T(8,128)(2,1)} copy(bf16[2,2560,384]{2,0,1:T(2,128)(2,1)} %all-gather.3.cloned.1.call-done) | data formatting | bytes 7864320 | tf_op jit(solution)/shard_map/all_gather | solution.py:69
  360.3 4.8 %fusion.15 = bf16[2,64,3,128]{3,1,2,0:T(8,128)(2,1)S(1)} fusion(bf16[2,2560,3,128]{1,3,2,0:T(8,128)(2,1)} %bitcast.73, f32[2,64,3,2560]{3,1,2,0:T(8,128)} %copy-done.1, f32[2,64,3]{1,2,0:T(4,128)S(1)} %broadcast_maximum_fusion, pred[2,2560]{1,0:T(4,128)(4,1)S(1)} %compare_or_fusion, f32[2,64,3]{1,2,0:T(4,128)S(1)} %fusion.2), kind=kOutput, calls=%fused_computation.13 | convolution fusion | flops 254705664 | bytes 7970816 | tf_op jit(solution)/shard_map/pqhk,pkhd->pqhd/dot_general | solution.py:86
  365.1 0.0 copy-start.7
  365.1 0.0 copy-start.3
  365.2 0.0 copy-start.6
  365.2 0.0 copy-start.8
  365.2 0.0 copy-start.5
  365.2 0.1 copy.64
  365.3 0.6 convolution_convert_fusion
  365.9 1.2 copy.69
  367.0 0.0 reduce-scatter.4.cloned.1.call-update
  367.1 36.4 %reduce-scatter.4.cloned.1.call-done = bf16[384,128]{1,0:T(8,128)(2,1)} async-done(((bf16[3072,128]{1,0:T(8,128)(2,1)}), bf16[384,128]{1,0:T(8,128)(2,1)}) %reduce-scatter.4.cloned.1.call-update) | async-done | bytes 98320
  403.5 1.0 copy.70
  404.5 0.7 add_convert_fusion
  405.2 3.3 all-to-all-start
  409.2 0.6 dynamic_slice.3
  409.9 2.9 all-to-all-done
  412.8 1.3 add_convert_fusion.3
  (21 shorter events, 0.2 us)
Async XLA Ops:
  7.2 358.1 %copy-start = (bf16[384,3072]{1,0:T(8,128)(2,1)S(1)}, bf16[384,3072]{1,0:T(8,128)(2,1)}, u32[]{:S(2)}) copy-start(bf16[384,3072]{1,0:T(8,128)(2,1)} %param.24) | copy-start | bytes 7077892
  7.2 13.2 %copy-start.4 = (bf16[1,2,16,384]{3,2,1,0:T(8,128)(2,1)S(1)}, bf16[1,2,16,384]{3,2,1,0:T(8,128)(2,1)}, u32[]{:S(2)}) copy-start(bf16[1,2,16,384]{3,2,1,0:T(8,128)(2,1)} %param.19) | copy-start | bytes 73732
  7.2 182.4 %all-gather.5.cloned.1.call-start = ((), (), s32[]{:S(2)}) async-start(), calls=%async_computation.3 | async-start | bytes 4055040 | tf_op jit(solution)/shard_map/all_gather | solution.py:68
  17.8 7.4 %copy-start.2 = (bf16[1,2,64,384]{3,2,1,0:T(8,128)(2,1)S(1)}, bf16[1,2,64,384]{3,2,1,0:T(8,128)(2,1)}, u32[]{:S(2)}) copy-start(bf16[1,2,64,384]{3,2,1,0:T(8,128)(2,1)} %param.18) | copy-start | bytes 294916
  25.2 324.6 %all-gather.3.cloned.1.call-start = ((), (), s32[]{:S(2)}) async-start(), calls=%async_computation.2 | async-start | bytes 4055040 | tf_op jit(solution)/shard_map/all_gather | solution.py:69
  27.0 376.5 %reduce-scatter.4.cloned.1.call-start = ((), (), s32[]{:S(2)}) async-start(), calls=%async_computation.4 | async-start | bytes 884736
  203.3 1.9 copy-start.1
  365.1 39.4 %copy-start.7 = (f32[384]{0:T(512)S(1)}, f32[384]{0:T(512)}, u32[]{:S(2)}) copy-start(f32[384]{0:T(512)} %param.25) | copy-start | bytes 4612
  365.1 39.4 %copy-start.3 = (bf16[1,2,64,384]{3,2,1,0:T(8,128)(2,1)S(1)}, bf16[1,2,64,384]{3,2,1,0:T(8,128)(2,1)}, u32[]{:S(2)}) copy-start(bf16[1,2,64,384]{3,2,1,0:T(8,128)(2,1)} %param.15) | copy-start | bytes 294916
  365.2 39.4 %copy-start.6 = (f32[1,2,384]{2,1,0:T(2,128)S(1)}, f32[1,2,384]{2,1,0:T(2,128)}, u32[]{:S(2)}) copy-start(f32[1,2,384]{2,1,0:T(2,128)} %param.23) | copy-start | bytes 9220
  365.2 44.1 %copy-start.8 = (f32[2]{0:T(128)S(1)}, f32[2]{0:T(128)}, u32[]{:S(2)}) copy-start(f32[2]{0:T(128)} %param.26) | copy-start | bytes 28
  365.2 47.7 %copy-start.5 = (bf16[1,64,384]{2,1,0:T(8,128)(2,1)S(1)}, bf16[1,64,384]{2,1,0:T(8,128)(2,1)}, u32[]{:S(2)}) copy-start(bf16[1,64,384]{2,1,0:T(8,128)(2,1)} %param.29) | copy-start | bytes 147460
  405.2 7.6 %all-to-all-start = ((bf16[1,2,64,384]{3,2,0,1:T(8,128)(2,1)}), bf16[1,2,64,384]{3,2,0,1:T(8,128)(2,1)S(1)}, u32[]{:S(2)}, u32[]{:S(2)}) async-start(bf16[1,2,64,384]{3,2,0,1:T(8,128)(2,1)} %add_convert_fusion), calls=%async_computation | async-start | bytes 196608 | tf_op jit(solution)/shard_map/all_to_all | solution.py:102
Sparse Core Ops, SparseCore 0:
  25.3 164.2 all-gather.4
  192.7 157.0 all-gather.2
  367.2 36.2 reduce-scatter.3
where the time goes:
time: 422 us; the launch traced here: 421 us
  waiting for transfers between devices  344 us (82%)
  local copies, waits for them, and re-layouts  35 us (8%)
  between operations  14.9 us (4%)
  other arithmetic  14.5 us (3%)
  matrix products  8.61 us (2%)
    all_gather x1, waiting for transfers between devices, shards(): key_piece = lax.all_gather(keys_local, 'seq', axis=1, tiled=True)  161 us
    all_gather x1, waiting for transfers between devices, shards(): value_piece = lax.all_gather(values_local, 'seq', axis=1, tiled=True)  144 us
    unnamed x4, waiting for transfers between devices  36.5 us
    all_gather x1, local copies, waits for them, and re-layouts, shards(): value_piece = lax.all_gather(values_local, 'seq', axis=1, tiled=True)  10.5 us
    all_gather x1, local copies, waits for them, and re-layouts, shards(): key_piece = lax.all_gather(keys_local, 'seq', axis=1, tiled=True)  10.5 us
  transfers between devices with their start and end apart: 4, of which 4 were waited for; matrix products, arithmetic and copies ran while one was open for 4% of the time, Pallas kernels for 0%

commit v1 on v0

--- a/solution.py
+++ b/solution.py
@@ -65,8 +65,13 @@
     keys_local = jnp.concatenate([keys_txt, keys_img], 1).reshape(prompts, slot_here, width_here)
     values_local = jnp.concatenate([txt_value[0], img_value[0]], 1)
     running = jnp.full((prompts, img_here, heads_here), -1e30, jnp.float32)
-    key_piece = lax.all_gather(keys_local, "seq", axis=1, tiled=True)
-    value_piece = lax.all_gather(values_local, "seq", axis=1, tiled=True)
+    key_piece, value_piece = jnp.split(
+        lax.all_gather(
+            jnp.concatenate([keys_local, values_local], axis=0), "seq", axis=1, tiled=True
+        ),
+        [keys_local.shape[0]],
+        axis=0,
+    )
     count = key_piece.shape[1]
     index = jnp.arange(count)
     device = index // slot_here

time: 422 us -> 326 us (0.77)
  waiting for transfers between devices: 344 us -> 230 us
  local copies, waits for them, and re-layouts: 35 us -> 48.3 us
    all_gather x2 -> x1, waiting for transfers between devices: 305 us -> 191 us  [shards(): lax.all_gather(jnp.concatenate([keys_local, values_local], axis=0), 'seq'...]
    unnamed x22 -> x26, local copies, waits for them, and re-layouts: 4.94 us -> 26.8 us
    all_gather x2 -> x0, local copies, waits for them, and re-layouts: 21.1 us -> none  [the longest x1 10.5 us: shards(): value_piece = lax.all_gather(values_local, 'seq', axis=1, tiled=True)]
    split x0 -> x1, local copies, waits for them, and re-layouts: none -> 11 us  [shards(): jnp.split(lax.all_gather(jnp.concatenate([keys_local, values_local], axis...]
    unnamed x4 -> x3, waiting for transfers between devices: 36.5 us -> 36.3 us
  transfers between devices with their start and end apart: 4 -> 3, of which waited for: 4 -> 3; matrix products, arithmetic and copies ran while one was open for 4% -> 1% of each run, Pallas kernels for 0% -> 0%
where the time goes in v1:
time: 326 us; the launch traced here: 324 us
  waiting for transfers between devices  230 us (71%)
  local copies, waits for them, and re-layouts  48.3 us (15%)
  other arithmetic  18.4 us (6%)
  between operations  15.1 us (5%)
  matrix products  9.21 us (3%)
  starting transfers between devices  3.42 us (1%)
    all_gather x1, waiting for transfers between devices, shards(): lax.all_gather(jnp.concatenate([keys_local, values_local], axis=0), 'seq'...  191 us
    unnamed x3, waiting for transfers between devices  36.3 us
    unnamed x26, local copies, waits for them, and re-layouts  26.8 us
    split x1, local copies, waits for them, and re-layouts, shards(): jnp.split(lax.all_gather(jnp.concatenate([keys_local, values_local], axis...  11 us
  transfers between devices with their start and end apart: 3, of which 3 were waited for; matrix products, arithmetic and copies ran while one was open for 1% of the time, Pallas kernels for 0%

profile of v1, /device:TPU:4, one launch (start us, length us, event | category | flops | bytes accessed | tf_op | source)
XLA Modules:
  0.0 324.2 jit_solution(14186076740903343891)
XLA Ops:
  7.2 0.0 copy-start
  7.2 0.0 all-gather.2.cloned.1.call-start
  7.2 1.7 convert_multiply_fusion.1
  9.0 1.0 copy.59
  10.0 1.6 convert_multiply_fusion.2
  11.6 1.0 copy.50
  12.6 0.6 fusion.35
  13.2 0.8 slice_bitcast_fusion.2
  14.0 0.8 mul.267
  14.7 1.4 mul.286
  16.2 0.7 convert_multiply_fusion
  16.9 0.1 reduce_sum.36
  17.1 0.1 div.90
  17.2 0.8 fusion.24
  18.0 0.8 copy.53
  18.8 1.7 copy.55
  20.5 1.6 copy.54
  22.0 1.0 mul.285
  23.0 0.2 reduce_sum.38
  23.3 0.1 copy.61
  23.4 1.0 mul.266
  24.4 0.8 reduce_sum.37
  25.2 1.5 add_sqrt_fusion.1
  26.8 0.9 copy.52
  27.7 0.8 broadcast_multiply_fusion.1
  28.5 0.2 fusion.26
  28.7 1.2 divide_multiply_fusion
  29.9 1.0 subtract_convert_fusion
  30.9 0.5 pad_maximum_fusion
  31.4 0.0 copy-done.2
  31.5 0.2 maximum_maximum_fusion
  31.7 0.9 copy.56
  32.6 0.0 all-gather.2.cloned.1.call-update
  32.6 0.0 reduce-scatter.4.cloned.1.call-start
  32.7 0.5 pad_maximum_fusion.1
  33.2 0.7 compare_or_fusion
  34.0 190.5 %all-gather.2.cloned.1.call-done = bf16[4,2560,384]{2,0,1:T(4,128)(2,1)} async-done(((bf16[4,80,384]{2,0,1:T(4,128)(2,1)}), bf16[4,2560,384]{2,0,1:T(4,128)(2,1)}) %all-gather.2.cloned.1.call-update) | async-done | bytes 7864336 | tf_op jit(solution)/shard_map/all_gather | solution.py:69
  224.5 11.0 %fusion.38 = (bf16[2,2560,384]{2,0,1:T(2,128)(2,1)}, bf16[2,2560,384]{2,0,1:T(2,128)(2,1)}) fusion(bf16[4,2560,384]{2,0,1:T(4,128)(2,1)} %all-gather.2.cloned.1.call-done), kind=kLoop, calls=%fused_computation.77 | loop fusion | bytes 15728640 | tf_op jit(solution)/shard_map/split | solution.py:68
  235.5 10.5 %copy.73 = bf16[2,2560,384]{1,2,0:T(8,128)(2,1)} copy(bf16[2,2560,384]{2,0,1:T(2,128)(2,1)} %get-tuple-element.2) | data formatting | bytes 7864320
  246.1 5.0 %fusion.39 = (f32[2,64,3]{1,2,0:T(4,128)S(1)}, f32[2,64,3,2560]{3,1,2,0:T(8,128)}) fusion(bf16[2,2560,3,128]{1,3,2,0:T(8,128)(2,1)} %bitcast.68, bf16[2,64,3,128]{1,3,2,0:T(8,128)(2,1)S(1)} %bitcast.77, pred[2,2560]{1,0:T(4,128)(4,1)S(1)} %compare_or_fusion), kind=kOutput, calls=%fused_computation.78 | convolution fusion | flops 254606976 | bytes 7969280 | tf_op jit(solution)/shard_map/pqhd,pkhd->pqhk/dot_general | solution.py:83
  251.1 10.5 %copy.72 = bf16[2,2560,384]{1,2,0:T(8,128)(2,1)} copy(bf16[2,2560,384]{2,0,1:T(2,128)(2,1)} %get-tuple-element.3) | data formatting | bytes 7864320
  261.6 3.1 fusion.2
  264.8 0.2 copy-done.1
  264.9 3.6 %fusion.15 = bf16[2,64,3,128]{3,1,2,0:T(8,128)(2,1)S(1)} fusion(bf16[2,2560,3,128]{1,3,2,0:T(8,128)(2,1)} %bitcast.69, f32[2,64,3,2560]{3,1,2,0:T(8,128)S(1)} %copy-done.1, f32[2,64,3]{1,2,0:T(4,128)S(1)} %broadcast_maximum_fusion, pred[2,2560]{1,0:T(4,128)(4,1)S(1)} %compare_or_fusion, f32[2,64,3]{1,2,0:T(4,128)S(1)} %fusion.2), kind=kOutput, calls=%fused_computation.13 | convolution fusion | flops 254705664 | bytes 7970816 | tf_op jit(solution)/shard_map/pqhk,pkhd->pqhd/dot_general | solution.py:91
  268.6 0.0 copy-start.8
  268.6 0.0 copy-start.5
  268.6 0.0 copy-start.7
  268.6 0.0 copy-start.9
  268.6 0.0 copy-start.6
  268.6 0.1 copy.65
  268.7 0.0 copy-done
  268.7 0.6 convolution_convert_fusion
  269.3 1.2 copy.70
  270.5 0.0 reduce-scatter.4.cloned.1.call-update
  270.5 36.2 %reduce-scatter.4.cloned.1.call-done = bf16[384,128]{1,0:T(8,128)(2,1)} async-done(((bf16[3072,128]{1,0:T(8,128)(2,1)}), bf16[384,128]{1,0:T(8,128)(2,1)}) %reduce-scatter.4.cloned.1.call-update) | async-done | bytes 98320
  306.8 1.0 copy.71
  307.8 0.0 copy-done.5
  307.8 0.0 copy-done.7
  307.8 0.7 add_convert_fusion
  308.5 3.3 %all-to-all-start = ((bf16[1,2,64,384]{3,2,0,1:T(8,128)(2,1)}), bf16[1,2,64,384]{3,2,0,1:T(8,128)(2,1)S(1)}, u32[]{:S(2)}, u32[]{:S(2)}) async-start(bf16[1,2,64,384]{3,2,0,1:T(8,128)(2,1)} %add_convert_fusion), calls=%async_computation | async-start | bytes 196608 | tf_op jit(solution)/shard_map/all_to_all | solution.py:107
  312.6 0.6 dynamic_slice.3
  313.2 2.9 all-to-all-done
  316.1 0.0 copy-done.6
  316.1 1.2 add_convert_fusion.3
  (20 shorter events, 0.2 us)
Async XLA Ops:
  7.2 261.6 %copy-start = (bf16[384,3072]{1,0:T(8,128)(2,1)S(1)}, bf16[384,3072]{1,0:T(8,128)(2,1)}, u32[]{:S(2)}) copy-start(bf16[384,3072]{1,0:T(8,128)(2,1)} %param.24) | copy-start | bytes 7077892
  7.2 217.3 %all-gather.2.cloned.1.call-start = ((), (), s32[]{:S(2)}) async-start(), calls=%async_computation.2 | async-start | bytes 8110080 | tf_op jit(solution)/shard_map/all_gather | solution.py:69
  25.2 6.2 %copy-start.2 = (bf16[2,16,384]{1,2,0:T(8,128)(2,1)S(1)}, bf16[2,16,384]{1,2,0:T(8,128)(2,1)}, u32[]{:S(2)}) copy-start(bf16[2,16,384]{1,2,0:T(8,128)(2,1)} %copy.53) | copy-start | bytes 73732
  25.2 6.2 %copy-start.3 = (bf16[1,2,64,384]{2,3,1,0:T(8,128)(2,1)S(1)}, bf16[1,2,64,384]{2,3,1,0:T(8,128)(2,1)}, u32[]{:S(2)}) copy-start(bf16[1,2,64,384]{2,3,1,0:T(8,128)(2,1)} %copy.55) | copy-start | bytes 294916
  27.7 3.8 %copy-start.4 = (bf16[1,2,16,384]{2,3,1,0:T(8,128)(2,1)S(1)}, bf16[1,2,16,384]{2,3,1,0:T(8,128)(2,1)}, u32[]{:S(2)}) copy-start(bf16[1,2,16,384]{2,3,1,0:T(8,128)(2,1)} %copy.54) | copy-start | bytes 73732
  32.6 274.1 %reduce-scatter.4.cloned.1.call-start = ((), (), s32[]{:S(2)}) async-start(), calls=%async_computation.3 | async-start | bytes 884736
  261.6 3.3 %copy-start.1 = (f32[2,64,3,2560]{3,1,2,0:T(8,128)S(1)}, f32[2,64,3,2560]{3,1,2,0:T(8,128)}, u32[]{:S(2)}) copy-start(f32[2,64,3,2560]{3,1,2,0:T(8,128)} %get-tuple-element.19) | copy-start | bytes 11796484
  268.6 39.2 %copy-start.8 = (f32[384]{0:T(512)S(1)}, f32[384]{0:T(512)}, u32[]{:S(2)}) copy-start(f32[384]{0:T(512)} %param.25) | copy-start | bytes 4612
  268.6 39.2 %copy-start.5 = (bf16[1,2,64,384]{3,2,1,0:T(8,128)(2,1)S(1)}, bf16[1,2,64,384]{3,2,1,0:T(8,128)(2,1)}, u32[]{:S(2)}) copy-start(bf16[1,2,64,384]{3,2,1,0:T(8,128)(2,1)} %param.15) | copy-start | bytes 294916
  268.6 39.2 %copy-start.7 = (f32[1,2,384]{2,1,0:T(2,128)S(1)}, f32[1,2,384]{2,1,0:T(2,128)}, u32[]{:S(2)}) copy-start(f32[1,2,384]{2,1,0:T(2,128)} %param.23) | copy-start | bytes 9220
  268.6 44.0 %copy-start.9 = (f32[2]{0:T(128)S(1)}, f32[2]{0:T(128)}, u32[]{:S(2)}) copy-start(f32[2]{0:T(128)} %param.26) | copy-start | bytes 28
  268.6 47.5 %copy-start.6 = (bf16[1,64,384]{2,1,0:T(8,128)(2,1)S(1)}, bf16[1,64,384]{2,1,0:T(8,128)(2,1)}, u32[]{:S(2)}) copy-start(bf16[1,64,384]{2,1,0:T(8,128)(2,1)} %param.29) | copy-start | bytes 147460
  308.5 7.6 %all-to-all-start = ((bf16[1,2,64,384]{3,2,0,1:T(8,128)(2,1)}), bf16[1,2,64,384]{3,2,0,1:T(8,128)(2,1)S(1)}, u32[]{:S(2)}, u32[]{:S(2)}) async-start(bf16[1,2,64,384]{3,2,0,1:T(8,128)(2,1)} %add_convert_fusion), calls=%async_computation | async-start | bytes 196608 | tf_op jit(solution)/shard_map/all_to_all | solution.py:107
Sparse Core Ops, SparseCore 0:
  32.7 191.6 all-gather.1
  270.6 36.0 reduce-scatter.3
